TPU v7x, 32 devices: a whole 2x2x4 slice. The times are simulated.
32 devices in a mesh: row: 8 (over z, y), col: 4 (over x, core).
Axes of the slice: x: 2, y: 2, z: 4, core: 2. Of those that a mesh axis runs over, the one named last changes fastest.
Arguments:
- anc_inverse: float32 [20480, 20480], P('row', 'col'), may hold values from -6 to 6
- l_store: float32 [4, 20480, 256], P('col', 'row'), may hold values from -0.0546875 to 0.0546875
- diag_inv: float32 [4, 256, 256], P('col'), may hold values from -6 to 6
- block_lists: int32 [4, 96], replicated, may hold values from 0 to 159, as said below
- block_counts: int32 [4], replicated, may hold values from 48 to 96, as said below
- sibling_columns: int32 [4], replicated, may hold values from 0 to 3, as said below
Outputs:
- upper_out: float32 [4, 256, 20480], P(None, 'row', 'col')
- lower_out: float32 [4, 20480, 256], P('col', 'row')
- diag_out: float32 [4, 256, 256], P('col')
Inputs may be any that keep to these rules, and one draw needn't show every extreme that they name: `block_lists`: in each sibling's row the entries are distinct block indices; entries at positions from block_counts onward are ignored. `block_counts`: some sibling uses all 96 entries. `sibling_columns`: distinct columns for distinct siblings.
All inputs are finite; a program needn't handle non-finite values.
Results may differ from a plain program's by a relative error of at most 0.00011.
Values sent between devices are 32-bit elements; how exact they have to be, the bound alone decides.
A program may use at most 128 MiB of HBM per device.

v0:
```python
import jax
import jax.numpy as jnp
from jax import lax
from jax.sharding import PartitionSpec as P

BLK = 128


def broadcast(block, axis, source):
    block = jnp.where(lax.axis_index(axis) == source, block, jnp.zeros_like(block))
    return lax.psum(block, axis)


def listed_blocks(block_lists, block_counts, first_block, block_total):
    block_ids = first_block + jnp.arange(block_total, dtype=jnp.int32)
    valid_entry = jnp.arange(block_lists.shape[1], dtype=jnp.int32)[None, :] < block_counts[:, None]
    entry_hits = (block_lists[:, :, None] == block_ids[None, None, :]) & valid_entry[:, :, None]
    return jnp.repeat(jnp.any(entry_hits, axis=1).astype(jnp.float32), BLK, axis=1)


def per_device(anc_inverse, l_store, diag_inv, block_lists, block_counts, sibling_columns):
    row_cells = anc_inverse.shape[0]
    col_cells = anc_inverse.shape[1]
    siblings = block_lists.shape[0]
    col_count = lax.axis_size("col")
    row_index = lax.axis_index("row")
    col_index = lax.axis_index("col")
    row_mask = listed_blocks(
        block_lists, block_counts, row_index * (row_cells // BLK), row_cells // BLK
    )
    col_mask = listed_blocks(
        block_lists, block_counts, col_index * (col_cells // BLK), col_cells // BLK
    )
    own_slot = l_store[0]
    chosen = (sibling_columns == col_index).astype(jnp.float32)
    stacked = jnp.stack(
        [broadcast(own_slot, "col", sibling_columns[sibling]) for sibling in range(siblings)]
    )
    masked = stacked * row_mask[:, :, None]
    partial_value = (
        -jnp.einsum(
            "jrw,rc->jwc",
            masked,
            anc_inverse,
            precision=lax.Precision.HIGHEST,
            preferred_element_type=jnp.float32,
        )
        * col_mask[:, None, :]
    )
    upper_part = lax.psum_scatter(partial_value, "row", scatter_dimension=1, tiled=True)
    owner_table = (
        sibling_columns[:, None] == jnp.arange(col_count, dtype=jnp.int32)[None, :]
    ).astype(jnp.float32)
    slots = jnp.einsum(
        "jc,jwt->wct",
        owner_table,
        upper_part,
        precision=lax.Precision.HIGHEST,
        preferred_element_type=jnp.float32,
    )
    slots = slots.reshape(slots.shape[0], col_count * col_cells)
    by_owner = lax.all_to_all(slots, "col", split_axis=1, concat_axis=1, tiled=True)
    picked = lax.all_to_all(by_owner, "row", split_axis=1, concat_axis=0, tiled=True)
    own_panel = jnp.sum(chosen[:, None, None] * masked, axis=0)
    inner_sum = jnp.dot(
        picked, own_panel, precision=lax.Precision.HIGHEST, preferred_element_type=jnp.float32
    )
    diag_total = lax.psum(inner_sum, "row")
    present = jnp.sum(chosen)
    diag_out = (present * diag_inv[0] - diag_total)[None]
    lower_out = jnp.transpose(picked)[None]
    return (upper_part, lower_out, diag_out)


def solution(mesh):
    return jax.shard_map(
        per_device,
        mesh=mesh,
        in_specs=(P("row", "col"), P("col", "row", None), P("col", None, None), P(), P(), P()),
        out_specs=(P(None, "row", "col"), P("col", "row", None), P("col", None, None)),
        check_vma=False,
    )
```

profile of v0, /device:TPU:0, one launch (start us, length us, event | category | flops | bytes accessed | tf_op | source)
XLA Modules:
  0.0 934.0 jit_solution(856084657477815547)
XLA Ops:
  7.2 0.0 all-reduce.6.cloned.1.call-start
  7.2 1.5 fusion.12
  11.3 6.0 broadcast_select_fusion.3
  17.3 0.0 copy-start.3
  17.3 0.0 copy-start.2
  17.3 0.0 all-reduce.6.cloned.1.call-update
  17.3 0.0 reduce-scatter.2.cloned.1.call-start
  17.4 0.6 copy-done.3
  17.9 0.1 iota_compare_fusion.1
  18.0 0.0 copy-done.2
  18.0 0.2 and_reduce_fusion
  18.2 0.1 broadcast_bitcast_fusion
  18.4 0.5 and_reduce_fusion.1
  18.9 0.1 copy.39
  19.0 0.1 broadcast_bitcast_fusion.1
  19.1 187.9 %all-reduce.6.cloned.1.call-done = (f32[1,2560,256]{2,1,0:T(8,128)}, f32[1,2560,256]{2,1,0:T(8,128)}, f32[1,2560,256]{2,1,0:T(8,128)}, f32[1,2560,256]{2,1,0:T(8,128)}) async-done(((f32[1,2560,256]{2,1,0:T(8,128)}, f32[1,2560,256]{2,1,0:T(8,128)}, f32[1,2560,256]{2,1,0:T(8,128)}, f32[1,2560,256]{2,1,0:T(8,128)}), (f32[1,2560,256]{2,1,0:T(8,128)}, f32[1,2560,256]{2,1,0:T(8,128)}, f32[1,2560,256]{2,1,0:T(8,128)}, ...) | async-done | bytes 10485776 | tf_op jit(solution)/shard_map/psum | solution.py:11
  207.0 188.3 %negate_multiply_fusion = f32[4,256,5120]{2,1,0:T(8,128)} fusion(f32[2560,5120]{1,0:T(8,128)} %param.6, f32[4,5120]{1,0:T(4,128)S(1)} %bitcast.44, f32[1,2560,256]{2,1,0:T(8,128)} %get-tuple-element.21, f32[1,2560,256]{2,1,0:T(8,128)} %get-tuple-element.22, f32[1,2560,256]{2,1,0:T(8,128)} %get-tuple-element.23, f32[1,2560,256]{2,1,0:T(8,128)} %get-tuple-element.24, ...), kind=kOutput, calls=%fused_computation.2 | convolution fusion | flops 161082245120 | bytes 84008960 | tf_op jit(solution)/shard_map/jrw,rc->jwc/dot_general | solution.py:41
  395.2 0.0 copy-start.1
  395.2 0.0 reduce-scatter.2.cloned.1.call-update
  395.3 342.8 %reduce-scatter.2.cloned.1.call-done = f32[4,32,5120]{2,1,0:T(8,128)} async-done(((f32[4,256,5120]{2,1,0:T(8,128)}), f32[4,32,5120]{2,1,0:T(8,128)}) %reduce-scatter.2.cloned.1.call-update) | async-done | bytes 2621456 | tf_op jit(solution)/shard_map/reduce_scatter | solution.py:50
  738.1 0.0 copy-done.1
  738.1 5.8 convolution_bitcast_fusion
  743.9 1.5 copy.42
  745.4 33.8 %all_to_all.25 = f32[32,4,5120]{2,0,1:T(8,128)S(1)} all-to-all(f32[32,4,5120]{2,0,1:T(8,128)S(1)} %copy.42), channel_id=1, replica_groups=mesh['row'=8,'col'=4] {'col'}, dimensions={1} | all-to-all | bytes 5242880 | tf_op jit(solution)/shard_map/all_to_all | solution.py:62
  779.2 1.7 copy.43
  780.9 2.1 all_to_all.19
  783.1 4.8 copy.44
  787.8 3.7 all-to-all-start.1
  791.6 0.0 all-reduce.4.cloned.1.call-start
  791.6 0.6 fusion.11
  792.2 7.0 multiply_reduce_fusion
  799.3 51.5 %all-to-all-done.1 = f32[32,8,2560]{2,0,1:T(8,128)S(1)} async-done(((f32[32,8,2560]{2,0,1:T(8,128)}), f32[32,8,2560]{2,0,1:T(8,128)S(1)}, u32[]{:S(2)}, u32[]{:S(2)}) %all-to-all-start.1) | async-done | bytes 2621472 | tf_op jit(solution)/shard_map/all_to_all | solution.py:63
  850.8 4.8 fusion.13
  855.5 0.0 all-reduce.4.cloned.1.call-update
  855.5 0.0 copy-start
  855.6 2.1 copy.45
  857.6 67.5 %all-reduce.4.cloned.1.call-done = f32[256,256]{1,0:T(8,128)} async-done(((f32[256,256]{1,0:T(8,128)}), f32[256,256]{1,0:T(8,128)}) %all-reduce.4.cloned.1.call-update) | async-done | bytes 262160 | tf_op jit(solution)/shard_map/psum | solution.py:68
  925.1 0.0 copy-done
  925.1 2.3 fusion.6
  (6 shorter events, 0.1 us)
Async XLA Ops:
  7.2 199.8 %all-reduce.6.cloned.1.call-start = ((), (), s32[]{:S(2)}) async-start(), calls=%async_computation.5 | async-start | bytes 20971520 | tf_op jit(solution)/shard_map/psum | solution.py:11
  17.3 0.7 copy-start.3
  17.3 0.7 copy-start.2
  17.3 720.8 %reduce-scatter.2.cloned.1.call-start = ((), (), s32[]{:S(2)}) async-start(), calls=%async_computation.3 | async-start | bytes 23592960 | tf_op jit(solution)/shard_map/reduce_scatter | solution.py:50
  395.2 342.9 %copy-start.1 = (s32[4]{0:T(128)S(1)}, s32[4]{0:T(128)}, u32[]{:S(2)}) copy-start(s32[4]{0:T(128)} %param.11) | copy-start | bytes 52
  787.8 62.9 %all-to-all-start.1 = ((f32[32,8,2560]{2,0,1:T(8,128)}), f32[32,8,2560]{2,0,1:T(8,128)S(1)}, u32[]{:S(2)}, u32[]{:S(2)}) async-start(f32[32,8,2560]{2,0,1:T(8,128)} %copy.44), calls=%async_computation.2 | async-start | bytes 5242880 | tf_op jit(solution)/shard_map/all_to_all | solution.py:63
  791.6 133.6 %all-reduce.4.cloned.1.call-start = ((), (), s32[]{:S(2)}) async-start(), calls=%async_computation.4 | async-start | bytes 524288 | tf_op jit(solution)/shard_map/psum | solution.py:68
  855.5 69.6 %copy-start = (f32[1,256,256]{2,1,0:T(8,128)S(1)}, f32[1,256,256]{2,1,0:T(8,128)}, u32[]{:S(2)}) copy-start(f32[1,256,256]{2,1,0:T(8,128)} %param.8) | copy-start | bytes 786436
Sparse Core Ops, SparseCore 0:
  17.4 189.5 all-reduce.5
  395.4 342.6 reduce-scatter.1
  855.7 69.4 all-reduce.3
where the time goes:
time: 934 us
  waiting for transfers between devices  650 us (70%)
  matrix products  199 us (21%)
  blocking collectives  33.8 us (4%)
  other arithmetic  16.7 us (2%)
  between operations  16.5 us (2%)
  local copies, waits for them, and re-layouts  14.6 us (2%)
    reduce_scatter x1, waiting for transfers between devices, per_device(): lax.psum_scatter(partial_value, 'row', scatter_dimension=1, tiled=True)  343 us
    dot_general x1, matrix products, per_device(): jnp.einsum('jrw,rc->jwc', masked, anc_inverse, precision=lax.Precision.HI...  188 us
    psum x1, waiting for transfers between devices, broadcast(): return lax.psum(block, axis)  188 us
    psum x1, waiting for transfers between devices, per_device(): diag_total = lax.psum(inner_sum, 'row')  67.5 us
    all_to_all x1, waiting for transfers between devices, per_device(): lax.all_to_all(by_owner, 'row', split_axis=1, concat_axis=0, tiled=True)  51.5 us
    all_to_all x1, blocking collectives, per_device(): lax.all_to_all(slots, 'col', split_axis=1, concat_axis=1, tiled=True)  33.8 us
  transfers between devices with their start and end apart: 4, of which 4 were waited for; matrix products, arithmetic and copies ran while one was open for 1% of the time, Pallas kernels for 0%

commit v1 on v0

--- a/solution.py
+++ b/solution.py
@@ -4,6 +4,22 @@
 from jax.sharding import PartitionSpec as P
 
 BLK = 128
+
+
+def _launch_body(page):
+    shard_axis = "row"
+    total_devices = lax.axis_size(shard_axis)
+
+    def guide_the_stages_all(k_now, s_next):
+        if s_next >= total_devices:
+            return k_now
+        e_now = tuple(((q, q ^ s_next) for q in range(total_devices)))
+        wide_out = lax.ppermute(k_now, shard_axis, e_now)
+        high = guide_the_stages_all(k_now + wide_out, 2 * s_next)
+        return high
+
+    all_values = guide_the_stages_all(page, 1)
+    return all_values
 
 
 def broadcast(block, axis, source):
@@ -65,7 +81,7 @@
     inner_sum = jnp.dot(
         picked, own_panel, precision=lax.Precision.HIGHEST, preferred_element_type=jnp.float32
     )
-    diag_total = lax.psum(inner_sum, "row")
+    diag_total = _launch_body(inner_sum)
     present = jnp.sum(chosen)
     diag_out = (present * diag_inv[0] - diag_total)[None]
     lower_out = jnp.transpose(picked)[None]

time: 934 us -> 891 us (0.954)
  waiting for transfers between devices: 650 us -> 602 us
    psum x1 -> x0, waiting for transfers between devices: 67.5 us -> none  [per_device(): diag_total = lax.psum(inner_sum, 'row')]
    ppermute x0 -> x3, waiting for transfers between devices: none -> 19.8 us  [guide_the_stages_all(): wide_out = lax.ppermute(k_now, shard_axis, e_now)]
  transfers between devices with their start and end apart: 4 -> 6, of which waited for: 4 -> 6; matrix products, arithmetic and copies ran while one was open for 1% -> 1% of each run, Pallas kernels for 0% -> 0%
where the time goes in v1:
time: 891 us
  waiting for transfers between devices  602 us (68%)
  matrix products  198 us (22%)
  blocking collectives  33.8 us (4%)
  between operations  16.7 us (2%)
  other arithmetic  15.7 us (2%)
  local copies, waits for them, and re-layouts  14.5 us (2%)
  starting transfers between devices  9.63 us (1%)
    reduce_scatter x1, waiting for transfers between devices, per_device(): lax.psum_scatter(partial_value, 'row', scatter_dimension=1, tiled=True)  343 us
    dot_general x1, matrix products, per_device(): jnp.einsum('jrw,rc->jwc', masked, anc_inverse, precision=lax.Precision.HI...  188 us
    psum x1, waiting for transfers between devices, broadcast(): return lax.psum(block, axis)  188 us
    all_to_all x1, waiting for transfers between devices, per_device(): lax.all_to_all(by_owner, 'row', split_axis=1, concat_axis=0, tiled=True)  51.6 us
    all_to_all x1, blocking collectives, per_device(): lax.all_to_all(slots, 'col', split_axis=1, concat_axis=1, tiled=True)  33.8 us
    ppermute x3, waiting for transfers between devices, guide_the_stages_all(): wide_out = lax.ppermute(k_now, shard_axis, e_now)  19.8 us
  transfers between devices with their start and end apart: 6, of which 6 were waited for; matrix products, arithmetic and copies ran while one was open for 1% of the time, Pallas kernels for 0%

profile of v1, /device:TPU:0, one launch (start us, length us, event | category | flops | bytes accessed | tf_op | source)
XLA Modules:
  0.0 891.0 jit_solution(14223723122934568616)
XLA Ops:
  7.2 0.0 all-reduce.3.cloned.1.call-start
  7.2 1.5 fusion.12
  11.3 5.9 broadcast_select_fusion.3
  17.2 0.0 copy-start.3
  17.2 0.0 copy-start.2
  17.2 0.0 all-reduce.3.cloned.1.call-update
  17.2 0.0 reduce-scatter.2.cloned.1.call-start
  17.3 0.6 copy-done.3
  17.8 0.1 iota_compare_fusion.1
  17.9 0.0 copy-done.2
  17.9 0.2 and_reduce_fusion
  18.1 0.1 broadcast_bitcast_fusion
  18.3 0.5 and_reduce_fusion.1
  18.8 0.1 copy.39
  18.9 0.1 broadcast_bitcast_fusion.1
  19.0 187.9 %all-reduce.3.cloned.1.call-done = (f32[1,2560,256]{2,1,0:T(8,128)}, f32[1,2560,256]{2,1,0:T(8,128)}, f32[1,2560,256]{2,1,0:T(8,128)}, f32[1,2560,256]{2,1,0:T(8,128)}) async-done(((f32[1,2560,256]{2,1,0:T(8,128)}, f32[1,2560,256]{2,1,0:T(8,128)}, f32[1,2560,256]{2,1,0:T(8,128)}, f32[1,2560,256]{2,1,0:T(8,128)}), (f32[1,2560,256]{2,1,0:T(8,128)}, f32[1,2560,256]{2,1,0:T(8,128)}, f32[1,2560,256]{2,1,0:T(8,128)}, ...) | async-done | bytes 10485776 | tf_op jit(solution)/shard_map/psum | solution.py:27
  206.9 188.3 %negate_multiply_fusion = f32[4,256,5120]{2,1,0:T(8,128)} fusion(f32[2560,5120]{1,0:T(8,128)} %param.6, f32[4,5120]{1,0:T(4,128)S(1)} %bitcast.44, f32[1,2560,256]{2,1,0:T(8,128)} %get-tuple-element.21, f32[1,2560,256]{2,1,0:T(8,128)} %get-tuple-element.22, f32[1,2560,256]{2,1,0:T(8,128)} %get-tuple-element.23, f32[1,2560,256]{2,1,0:T(8,128)} %get-tuple-element.24, ...), kind=kOutput, calls=%fused_computation.2 | convolution fusion | flops 161082245120 | bytes 84008960 | tf_op jit(solution)/shard_map/jrw,rc->jwc/dot_general | solution.py:57
  395.2 0.0 copy-start.1
  395.2 0.0 reduce-scatter.2.cloned.1.call-update
  395.2 343.1 %reduce-scatter.2.cloned.1.call-done = f32[4,32,5120]{2,1,0:T(8,128)} async-done(((f32[4,256,5120]{2,1,0:T(8,128)}), f32[4,32,5120]{2,1,0:T(8,128)}) %reduce-scatter.2.cloned.1.call-update) | async-done | bytes 2621456 | tf_op jit(solution)/shard_map/reduce_scatter | solution.py:66
  738.4 0.0 copy-done.1
  738.4 5.8 convolution_bitcast_fusion
  744.1 1.5 copy.42
  745.7 33.8 %all_to_all.25 = f32[32,4,5120]{2,0,1:T(8,128)S(1)} all-to-all(f32[32,4,5120]{2,0,1:T(8,128)S(1)} %copy.42), channel_id=1, replica_groups=mesh['row'=8,'col'=4] {'col'}, dimensions={1} | all-to-all | bytes 5242880 | tf_op jit(solution)/shard_map/all_to_all | solution.py:78
  779.5 1.7 copy.43
  781.2 2.1 all_to_all.19
  783.3 4.8 copy.44
  788.1 3.8 all-to-all-start.1
  791.9 0.7 fusion.11
  792.6 6.8 multiply_reduce_fusion
  799.4 51.6 %all-to-all-done.1 = f32[32,8,2560]{2,0,1:T(8,128)S(1)} async-done(((f32[32,8,2560]{2,0,1:T(8,128)}), f32[32,8,2560]{2,0,1:T(8,128)S(1)}, u32[]{:S(2)}, u32[]{:S(2)}) %all-to-all-start.1) | async-done | bytes 2621472 | tf_op jit(solution)/shard_map/all_to_all | solution.py:79
  851.0 4.0 fusion.13
  855.1 1.5 collective-permute-start
  856.6 5.6 collective-permute-done
  862.2 0.8 collective-permute-start.1
  863.0 5.6 collective-permute-done.1
  868.7 3.3 collective-permute-start.2
  872.1 0.0 copy-start
  872.1 2.1 copy.45
  874.1 8.6 collective-permute-done.2
  882.7 0.0 copy-done
  882.7 1.4 fusion.6
  (8 shorter events, 0.1 us)
Async XLA Ops:
  7.2 199.7 %all-reduce.3.cloned.1.call-start = ((), (), s32[]{:S(2)}) async-start(), calls=%async_computation.4 | async-start | bytes 20971520 | tf_op jit(solution)/shard_map/psum | solution.py:27
  17.2 0.7 copy-start.3
  17.2 0.7 copy-start.2
  17.2 721.1 %reduce-scatter.2.cloned.1.call-start = ((), (), s32[]{:S(2)}) async-start(), calls=%async_computation.3 | async-start | bytes 23592960 | tf_op jit(solution)/shard_map/reduce_scatter | solution.py:66
  395.2 343.2 %copy-start.1 = (s32[4]{0:T(128)S(1)}, s32[4]{0:T(128)}, u32[]{:S(2)}) copy-start(s32[4]{0:T(128)} %param.11) | copy-start | bytes 52
  788.1 62.9 %all-to-all-start.1 = ((f32[32,8,2560]{2,0,1:T(8,128)}), f32[32,8,2560]{2,0,1:T(8,128)S(1)}, u32[]{:S(2)}, u32[]{:S(2)}) async-start(f32[32,8,2560]{2,0,1:T(8,128)} %copy.44), calls=%async_computation.2 | async-start | bytes 5242880 | tf_op jit(solution)/shard_map/all_to_all | solution.py:79
  855.1 7.1 collective-permute-start
  862.2 6.5 collective-permute-start.1
  868.7 14.0 %collective-permute-start.2 = (f32[256,256]{1,0:T(8,128)S(1)}, f32[256,256]{1,0:T(8,128)S(1)}, u32[]{:S(2)}, u32[]{:S(2)}) collective-permute-start(f32[256,256]{1,0:T(8,128)S(1)} %add.44), channel_id=1, source_target_pairs={{0,16},{4,20},{8,24},{12,28},{16,0},{20,4},{24,8},{28,12},{1,17},{... | collective-permute-start | bytes 786440 | tf_op jit(solution)/shard_map/ppermute | solution.py:17
  872.1 10.7 %copy-start = (f32[1,256,256]{2,1,0:T(8,128)S(1)}, f32[1,256,256]{2,1,0:T(8,128)}, u32[]{:S(2)}) copy-start(f32[1,256,256]{2,1,0:T(8,128)} %param.8) | copy-start | bytes 786436
Sparse Core Ops, SparseCore 0:
  17.3 189.5 all-reduce.2
  395.4 342.9 reduce-scatter.1
